TPU v7x, 1024 devices: a whole 8x8x8 slice. The times are simulated.
1024 devices in a mesh: seq: 128 (over z, x, core), head: 8 (over y).
Axes of the slice: x: 8, y: 8, z: 8, core: 2. Of those that a mesh axis runs over, the one named last changes fastest.
Arguments:
- history: bfloat16 [98304, 1024], P('seq'), may hold values from -6 to 6
- ln_gain: bfloat16 [1024], replicated, may hold values from 0.5 to 1.5
- w_in: bfloat16 [4, 1024, 1024], P(None, None, 'head'), may hold values from -0.1875 to 0.1875
- out_gain: bfloat16 [1024], P('head'), may hold values from 0.5 to 1.5
- w_out: bfloat16 [1024, 1024], P('head'), may hold values from -0.25 to 0.25
- block_lists: int32 [768, 16], P('seq'), may hold values from 0 to 767, as said below
- counts: int32 [768], P('seq'), may hold values from 1 to 16, as said below
Outputs:
- mixed: bfloat16 [98304, 1024], P('seq', 'head')
Inputs may be any that keep to these rules, and one draw needn't show every extreme that they name: For query block b, entries 0 to counts[b] - 1 of block_lists[b] are distinct blocks from max(0, b - 31) to b, and entry 0 is b itself; later entries equal b and are not live. counts[b] is at most min(16, b + 1); the last block has min(16, 32, 768) live entries.
All inputs are finite; a program needn't handle non-finite values.
Results may differ from a plain program's by a relative error of at most 0.008.
Values may be sent and summed in bfloat16 or wider, within the bound.
A program may use at most 64 MiB of HBM per device.

v0:
```python
import jax
import jax.numpy as jnp
from jax import lax
from jax.sharding import PartitionSpec as P

DH = 128
WIN = 32
MAXK = 16


EPS = 1e-05


def shifted(shard, axis, by):
    length = lax.axis_size(axis)
    pairs = [(i, i + by) for i in range(length) if 0 <= i + by < length]
    return lax.ppermute(shard, axis, pairs)


def body(history, ln_gain, w_in, out_gain, w_out, block_lists, counts):
    tok_rows, width = history.shape
    blocks_dev = counts.shape[0]
    block_rows = tok_rows // blocks_dev
    head_cols = w_in.shape[2]
    heads_dev = head_cols // DH
    scale = DH ** (-0.5)
    floats = history.astype(jnp.float32)
    centre = jnp.mean(floats, axis=-1, keepdims=True)
    spread_sq = jnp.mean(jnp.square(floats - centre), axis=-1, keepdims=True)
    normed_x = (
        (floats - centre) * lax.rsqrt(spread_sq + EPS) * ln_gain.astype(jnp.float32)
    ).astype(jnp.bfloat16)
    projected = jnp.einsum("td,pde->pte", normed_x, w_in, preferred_element_type=jnp.float32)
    projected = jax.nn.silu(projected).astype(jnp.bfloat16)
    gating = projected[0]
    queries = projected[2]
    keys_values = jnp.stack([projected[3], projected[1]])
    seq_index = lax.axis_index("seq")
    reach_devs = (WIN - 1 + blocks_dev - 1) // blocks_dev
    depth = reach_devs + 1

    def advance(carried, unused):
        arrived = shifted(carried, "seq", 1)
        return (arrived, arrived)

    last_one, earlier = lax.scan(advance, keys_values, None, length=reach_devs)
    window = jnp.concatenate([keys_values[None], earlier], axis=0)
    in_list = jnp.arange(MAXK, dtype=jnp.int32)[None, :] < counts[:, None]
    queries_h = queries.reshape(tok_rows, heads_dev, DH)
    rows_here = jnp.arange(tok_rows, dtype=jnp.int32)

    def visit(attended, item):
        visiting, offset = item
        source = seq_index - offset
        key_ids = source * blocks_dev + jnp.arange(blocks_dev, dtype=jnp.int32)
        member = jnp.any(
            in_list[:, :, None] & (block_lists[:, :, None] == key_ids[None, None, :]), axis=1
        )
        member_rows = jnp.broadcast_to(
            member[:, None, :, None], (blocks_dev, block_rows, blocks_dev, block_rows)
        )
        member_rows = member_rows.reshape(tok_rows, tok_rows)
        causal = (source * tok_rows + rows_here)[None, :] <= (seq_index * tok_rows + rows_here)[
            :, None
        ]
        allowed = member_rows & causal
        visit_keys = visiting[0].reshape(tok_rows, heads_dev, DH)
        visit_values = visiting[1].reshape(tok_rows, heads_dev, DH)
        scores = (
            jnp.einsum("qhe,khe->hqk", queries_h, visit_keys, preferred_element_type=jnp.float32)
            * scale
        )
        weights = jnp.where(allowed[None], jax.nn.silu(scores), 0.0).astype(jnp.bfloat16)
        update = jnp.einsum(
            "hqk,khe->qhe", weights, visit_values, preferred_element_type=jnp.float32
        )
        return (attended + update, None)

    start = jnp.zeros((tok_rows, heads_dev, DH), jnp.float32)
    attended, unused = lax.scan(visit, start, (window, jnp.arange(depth, dtype=jnp.int32)))
    centre_h = jnp.mean(attended, axis=-1, keepdims=True)
    spread_h = jnp.mean(jnp.square(attended - centre_h), axis=-1, keepdims=True)
    normed_h = (attended - centre_h) * lax.rsqrt(spread_h + EPS)
    gated = (
        normed_h
        * out_gain.astype(jnp.float32).reshape(heads_dev, DH)
        * gating.astype(jnp.float32).reshape(tok_rows, heads_dev, DH)
    )
    gated = gated.astype(jnp.bfloat16).reshape(tok_rows, head_cols)
    partial_terms = jnp.dot(gated, w_out, preferred_element_type=jnp.float32)
    summed = lax.psum_scatter(partial_terms, "head", scatter_dimension=1, tiled=True)
    columns = width // lax.axis_size("head")
    residual = lax.dynamic_slice_in_dim(history, lax.axis_index("head") * columns, columns, 1)
    return (summed + residual.astype(jnp.float32)).astype(jnp.bfloat16)


def solution(mesh):
    placed = (
        P("seq", None),
        P(),
        P(None, None, "head"),
        P("head"),
        P("head", None),
        P("seq", None),
        P("seq"),
    )
    return jax.shard_map(
        body, mesh=mesh, in_specs=placed, out_specs=P("seq", "head"), check_vma=False
    )
```

profile of v0, /device:TPU:14, one launch (start us, length us, event | category | flops | bytes accessed | tf_op | source)
XLA Modules:
  0.0 213.8 jit_solution(12268272713446211364)
XLA Ops:
  6.6 1.8 convert_reduce_fusion
  9.1 1.3 fusion.38
  10.4 0.9 copy-done.2
  11.3 0.7 slice_bitcast_fusion.2
  12.0 0.8 fusion.48
  12.8 68.2 %while.25 = (s32[]{:T(128)}, bf16[2,768,128]{2,1,0:T(8,128)(2,1)}, bf16[6,2,768,128]{3,2,1,0:T(8,128)(2,1)}, s32[]{:T(128)}) while((s32[]{:T(128)}, bf16[2,768,128]{2,1,0:T(8,128)(2,1)}, bf16[6,2,768,128]{3,2,1,0:T(8,128)(2,1)}, s32[]{:T(128)}) %tuple.49), condition=%wide.region_3.4_spmd, body=%wide.region_2.3_spmd.sunk | while | flops 2 | bytes 3145833 | solution.py:46
  12.8 1.9 collective-permute-start
  14.7 7.4 %collective-permute-done = bf16[2,768,128]{2,1,0:T(8,128)(2,1)S(1)} collective-permute-done((bf16[2,768,128]{2,1,0:T(8,128)(2,1)}, bf16[2,768,128]{2,1,0:T(8,128)(2,1)S(1)}, u32[]{:S(2)}, u32[]{:S(2)}) %collective-permute-start) | collective-permute-done | bytes 393248 | tf_op jit(solution)/shard_map/while/body/eval_jaxpr/ppermute | solution.py:17
  22.1 0.7 copy.29
  22.8 0.8 bitcast_dynamic-update-slice_fusion.2
  23.6 2.7 %collective-permute-start = (bf16[2,768,128]{2,1,0:T(8,128)(2,1)}, bf16[2,768,128]{2,1,0:T(8,128)(2,1)S(1)}, u32[]{:S(2)}, u32[]{:S(2)}) collective-permute-start(bf16[2,768,128]{2,1,0:T(8,128)(2,1)} %get-tuple-element.297), channel_id=1, source_target_pairs={{0,8},{8,16},{16,24},{24,32},{32,40},{40,48},{48,56},{56,64},{64,7... | collective-permute-start | bytes 1179656 | tf_op jit(solution)/shard_map/while/body/eval_jaxpr/ppermute | solution.py:17
  26.3 6.6 %collective-permute-done = bf16[2,768,128]{2,1,0:T(8,128)(2,1)S(1)} collective-permute-done((bf16[2,768,128]{2,1,0:T(8,128)(2,1)}, bf16[2,768,128]{2,1,0:T(8,128)(2,1)S(1)}, u32[]{:S(2)}, u32[]{:S(2)}) %collective-permute-start) | collective-permute-done | bytes 393248 | tf_op jit(solution)/shard_map/while/body/eval_jaxpr/ppermute | solution.py:17
  32.9 0.7 copy.29
  33.6 0.8 bitcast_dynamic-update-slice_fusion.2
  34.4 4.8 %collective-permute-start = (bf16[2,768,128]{2,1,0:T(8,128)(2,1)}, bf16[2,768,128]{2,1,0:T(8,128)(2,1)S(1)}, u32[]{:S(2)}, u32[]{:S(2)}) collective-permute-start(bf16[2,768,128]{2,1,0:T(8,128)(2,1)} %get-tuple-element.297), channel_id=1, source_target_pairs={{0,8},{8,16},{16,24},{24,32},{32,40},{40,48},{48,56},{56,64},{64,7... | collective-permute-start | bytes 1179656 | tf_op jit(solution)/shard_map/while/body/eval_jaxpr/ppermute | solution.py:17
  39.2 4.5 %collective-permute-done = bf16[2,768,128]{2,1,0:T(8,128)(2,1)S(1)} collective-permute-done((bf16[2,768,128]{2,1,0:T(8,128)(2,1)}, bf16[2,768,128]{2,1,0:T(8,128)(2,1)S(1)}, u32[]{:S(2)}, u32[]{:S(2)}) %collective-permute-start) | collective-permute-done | bytes 393248 | tf_op jit(solution)/shard_map/while/body/eval_jaxpr/ppermute | solution.py:17
  43.7 0.7 copy.29
  44.4 0.8 bitcast_dynamic-update-slice_fusion.2
  45.2 6.9 %collective-permute-start = (bf16[2,768,128]{2,1,0:T(8,128)(2,1)}, bf16[2,768,128]{2,1,0:T(8,128)(2,1)S(1)}, u32[]{:S(2)}, u32[]{:S(2)}) collective-permute-start(bf16[2,768,128]{2,1,0:T(8,128)(2,1)} %get-tuple-element.297), channel_id=1, source_target_pairs={{0,8},{8,16},{16,24},{24,32},{32,40},{40,48},{48,56},{56,64},{64,7... | collective-permute-start | bytes 1179656 | tf_op jit(solution)/shard_map/while/body/eval_jaxpr/ppermute | solution.py:17
  52.1 2.3 %collective-permute-done = bf16[2,768,128]{2,1,0:T(8,128)(2,1)S(1)} collective-permute-done((bf16[2,768,128]{2,1,0:T(8,128)(2,1)}, bf16[2,768,128]{2,1,0:T(8,128)(2,1)S(1)}, u32[]{:S(2)}, u32[]{:S(2)}) %collective-permute-start) | collective-permute-done | bytes 393248 | tf_op jit(solution)/shard_map/while/body/eval_jaxpr/ppermute | solution.py:17
  54.5 0.7 copy.29
  55.2 0.8 bitcast_dynamic-update-slice_fusion.2
  56.0 9.0 %collective-permute-start = (bf16[2,768,128]{2,1,0:T(8,128)(2,1)}, bf16[2,768,128]{2,1,0:T(8,128)(2,1)S(1)}, u32[]{:S(2)}, u32[]{:S(2)}) collective-permute-start(bf16[2,768,128]{2,1,0:T(8,128)(2,1)} %get-tuple-element.297), channel_id=1, source_target_pairs={{0,8},{8,16},{16,24},{24,32},{32,40},{40,48},{48,56},{56,64},{64,7... | collective-permute-start | bytes 1179656 | tf_op jit(solution)/shard_map/while/body/eval_jaxpr/ppermute | solution.py:17
  65.0 1.5 collective-permute-done
  66.6 0.7 copy.29
  67.3 0.8 bitcast_dynamic-update-slice_fusion.2
  68.1 9.9 %collective-permute-start = (bf16[2,768,128]{2,1,0:T(8,128)(2,1)}, bf16[2,768,128]{2,1,0:T(8,128)(2,1)S(1)}, u32[]{:S(2)}, u32[]{:S(2)}) collective-permute-start(bf16[2,768,128]{2,1,0:T(8,128)(2,1)} %get-tuple-element.297), channel_id=1, source_target_pairs={{0,8},{8,16},{16,24},{24,32},{32,40},{40,48},{48,56},{56,64},{64,7... | collective-permute-start | bytes 1179656 | tf_op jit(solution)/shard_map/while/body/eval_jaxpr/ppermute | solution.py:17
  77.9 1.5 collective-permute-done
  79.5 0.7 copy.29
  80.2 0.8 bitcast_dynamic-update-slice_fusion.2
  81.0 3.5 %pad_maximum_fusion = bf16[7,2,768,128]{3,2,1,0:T(8,128)(2,1)} fusion(bf16[6,2,768,128]{3,2,1,0:T(8,128)(2,1)} %get-tuple-element.113, bf16[1,2,768,128]{3,2,1,0:T(8,128)(2,1)S(1)} %get-tuple-element.212), kind=kLoop, calls=%fused_computation.38 | loop fusion | flops 1376256 | bytes 5505024 | tf_op jit(solution)/shard_map/concatenate | solution.py:47
  84.5 42.8 %while.26 = (s32[]{:T(128)}, f32[768,1,128]{0,2,1:T(8,128)}, bf16[7,2,768,128]{3,2,1,0:T(8,128)(2,1)}, s32[6,16]{1,0:T(8,128)S(1)}, s32[7]{0:T(128)S(1)}, /*inde...) while((s32[]{:T(128)}, f32[768,1,128]{0,2,1:T(8,128)}, ...), condition=%wide.region_6.7_spmd.clone.clone, body=%wide.region_4.6_spmd.clone.clone.sunk | while | flops 307498240 | bytes 4929451 | solution.py:80
  87.4 3.2 %fusion.54 = f32[768,1,128]{0,2,1:T(8,128)} fusion(pred[768,768]{0,1:T(32,128)(4,1)S(1)} %copy.20, s32[768]{0:T(1024)S(1)} %get-tuple-element.290, s32[768]{0:T(1024)S(1)} %get-tuple-element.291, f32[768,1,128]{0,2,1:T(8,128)} %get-tuple-element.319, bf16[7,2,768,128]{3,2,1,0:T(8,128)(2,1)} %get-tuple-element.334, s32[]{:T(128)} %get-tuple-element.318, ...), kind=kOutput, calls=%fused_computation.13.clone.1 | convolution fusion | flops 307494912 | bytes 1973253 | tf_op jit(solution)/shard_map/while/body/eval_jaxpr/hqk,khe->qhe/dot_general | solution.py:74
  92.6 0.7 copy.20
  93.3 3.3 %fusion.54 = f32[768,1,128]{0,2,1:T(8,128)} fusion(pred[768,768]{0,1:T(32,128)(4,1)S(1)} %copy.20, s32[768]{0:T(1024)S(1)} %get-tuple-element.290, s32[768]{0:T(1024)S(1)} %get-tuple-element.291, f32[768,1,128]{0,2,1:T(8,128)} %get-tuple-element.319, bf16[7,2,768,128]{3,2,1,0:T(8,128)(2,1)} %get-tuple-element.334, s32[]{:T(128)} %get-tuple-element.318, ...), kind=kOutput, calls=%fused_computation.13.clone.1 | convolution fusion | flops 307494912 | bytes 1973253 | tf_op jit(solution)/shard_map/while/body/eval_jaxpr/hqk,khe->qhe/dot_general | solution.py:74
  98.8 0.7 copy.20
  99.5 3.3 %fusion.54 = f32[768,1,128]{0,2,1:T(8,128)} fusion(pred[768,768]{0,1:T(32,128)(4,1)S(1)} %copy.20, s32[768]{0:T(1024)S(1)} %get-tuple-element.290, s32[768]{0:T(1024)S(1)} %get-tuple-element.291, f32[768,1,128]{0,2,1:T(8,128)} %get-tuple-element.319, bf16[7,2,768,128]{3,2,1,0:T(8,128)(2,1)} %get-tuple-element.334, s32[]{:T(128)} %get-tuple-element.318, ...), kind=kOutput, calls=%fused_computation.13.clone.1 | convolution fusion | flops 307494912 | bytes 1973253 | tf_op jit(solution)/shard_map/while/body/eval_jaxpr/hqk,khe->qhe/dot_general | solution.py:74
  104.9 0.7 copy.20
  105.6 3.3 %fusion.54 = f32[768,1,128]{0,2,1:T(8,128)} fusion(pred[768,768]{0,1:T(32,128)(4,1)S(1)} %copy.20, s32[768]{0:T(1024)S(1)} %get-tuple-element.290, s32[768]{0:T(1024)S(1)} %get-tuple-element.291, f32[768,1,128]{0,2,1:T(8,128)} %get-tuple-element.319, bf16[7,2,768,128]{3,2,1,0:T(8,128)(2,1)} %get-tuple-element.334, s32[]{:T(128)} %get-tuple-element.318, ...), kind=kOutput, calls=%fused_computation.13.clone.1 | convolution fusion | flops 307494912 | bytes 1973253 | tf_op jit(solution)/shard_map/while/body/eval_jaxpr/hqk,khe->qhe/dot_general | solution.py:74
  111.0 0.7 copy.20
  111.8 3.3 %fusion.54 = f32[768,1,128]{0,2,1:T(8,128)} fusion(pred[768,768]{0,1:T(32,128)(4,1)S(1)} %copy.20, s32[768]{0:T(1024)S(1)} %get-tuple-element.290, s32[768]{0:T(1024)S(1)} %get-tuple-element.291, f32[768,1,128]{0,2,1:T(8,128)} %get-tuple-element.319, bf16[7,2,768,128]{3,2,1,0:T(8,128)(2,1)} %get-tuple-element.334, s32[]{:T(128)} %get-tuple-element.318, ...), kind=kOutput, calls=%fused_computation.13.clone.1 | convolution fusion | flops 307494912 | bytes 1973253 | tf_op jit(solution)/shard_map/while/body/eval_jaxpr/hqk,khe->qhe/dot_general | solution.py:74
  117.9 3.3 %fusion.54 = f32[768,1,128]{0,2,1:T(8,128)} fusion(pred[768,768]{0,1:T(32,128)(4,1)S(1)} %copy.20, s32[768]{0:T(1024)S(1)} %get-tuple-element.290, s32[768]{0:T(1024)S(1)} %get-tuple-element.291, f32[768,1,128]{0,2,1:T(8,128)} %get-tuple-element.319, bf16[7,2,768,128]{3,2,1,0:T(8,128)(2,1)} %get-tuple-element.334, s32[]{:T(128)} %get-tuple-element.318, ...), kind=kOutput, calls=%fused_computation.13.clone.1 | convolution fusion | flops 307494912 | bytes 1973253 | tf_op jit(solution)/shard_map/while/body/eval_jaxpr/hqk,khe->qhe/dot_general | solution.py:74
  124.0 3.3 %fusion.54 = f32[768,1,128]{0,2,1:T(8,128)} fusion(pred[768,768]{0,1:T(32,128)(4,1)S(1)} %copy.20, s32[768]{0:T(1024)S(1)} %get-tuple-element.290, s32[768]{0:T(1024)S(1)} %get-tuple-element.291, f32[768,1,128]{0,2,1:T(8,128)} %get-tuple-element.319, bf16[7,2,768,128]{3,2,1,0:T(8,128)(2,1)} %get-tuple-element.334, s32[]{:T(128)} %get-tuple-element.318, ...), kind=kOutput, calls=%fused_computation.13.clone.1 | convolution fusion | flops 307494912 | bytes 1973253 | tf_op jit(solution)/shard_map/while/body/eval_jaxpr/hqk,khe->qhe/dot_general | solution.py:74
  127.4 1.1 copy.13
  128.5 1.0 reduce_sum.38
  129.9 3.2 %fusion.43 = f32[768,1024]{1,0:T(8,128)} fusion(bf16[128,1024]{1,0:T(8,128)(2,1)S(1)} %copy-done.3, f32[768,1,128]{2,0,1:T(8,128)S(1)} %copy.13, bf16[4,768,128]{2,1,0:T(8,128)(2,1)} %copy-done.2, f32[128]{0:T(128)S(1)} %convert_element_type.46, f32[768]{0:T(1024)S(1)} %add_rsqrt_fusion, f32[768]{0:T(1024)S(1)} %broadcast_multiply_fusion), kind=kOutput, calls=%fused_computation.56 | convolution fusion | flops 201916416 | bytes 4004352 | tf_op jit(solution)/shard_map/dot_general | solution.py:90
  133.2 72.0 %reduce-scatter.2.cloned.1.call-done = f32[768,128]{1,0:T(8,128)} async-done(((f32[768,1024]{1,0:T(8,128)}), f32[768,128]{1,0:T(8,128)}) %reduce-scatter.2.cloned.1.call-update) | async-done | bytes 393232 | tf_op jit(solution)/shard_map/reduce_scatter | solution.py:91
  205.2 1.7 add_convert_fusion
  (80 shorter events, 13.6 us)
Async XLA Ops:
  6.5 2.6 %copy-start = (bf16[4,1024,128]{2,1,0:T(8,128)(2,1)S(1)}, bf16[4,1024,128]{2,1,0:T(8,128)(2,1)}, u32[]{:S(2)}) copy-start(bf16[4,1024,128]{2,1,0:T(8,128)(2,1)} %param.13) | copy-start | bytes 3145732
  6.5 2.0 copy-start.1
  6.5 2.5 %copy-start.5 = (bf16[1024]{0:T(1024)(128)(2,1)S(1)}, bf16[1024]{0:T(1024)(128)(2,1)}, u32[]{:S(2)}) copy-start(bf16[1024]{0:T(1024)(128)(2,1)} %param.12) | copy-start | bytes 6148
  6.5 198.7 %reduce-scatter.2.cloned.1.call-start = ((), (), s32[]{:S(2)}) async-start(), calls=%async_computation.1 | async-start | bytes 3538944 | tf_op jit(solution)/shard_map/reduce_scatter | solution.py:91
  10.4 0.9 copy-start.2
  12.8 9.3 %collective-permute-start = (bf16[2,768,128]{2,1,0:T(8,128)(2,1)}, bf16[2,768,128]{2,1,0:T(8,128)(2,1)S(1)}, u32[]{:S(2)}, u32[]{:S(2)}) collective-permute-start(bf16[2,768,128]{2,1,0:T(8,128)(2,1)} %get-tuple-element.297), channel_id=1, source_target_pairs={{0,8},{8,16},{16,24},{24,32},{32,40},{40,48},{48,56},{56,64},{64,7... | collective-permute-start | bytes 1179656 | tf_op jit(solution)/shard_map/while/body/eval_jaxpr/ppermute | solution.py:17
  23.6 9.3 %collective-permute-start = (bf16[2,768,128]{2,1,0:T(8,128)(2,1)}, bf16[2,768,128]{2,1,0:T(8,128)(2,1)S(1)}, u32[]{:S(2)}, u32[]{:S(2)}) collective-permute-start(bf16[2,768,128]{2,1,0:T(8,128)(2,1)} %get-tuple-element.297), channel_id=1, source_target_pairs={{0,8},{8,16},{16,24},{24,32},{32,40},{40,48},{48,56},{56,64},{64,7... | collective-permute-start | bytes 1179656 | tf_op jit(solution)/shard_map/while/body/eval_jaxpr/ppermute | solution.py:17
  34.4 9.3 %collective-permute-start = (bf16[2,768,128]{2,1,0:T(8,128)(2,1)}, bf16[2,768,128]{2,1,0:T(8,128)(2,1)S(1)}, u32[]{:S(2)}, u32[]{:S(2)}) collective-permute-start(bf16[2,768,128]{2,1,0:T(8,128)(2,1)} %get-tuple-element.297), channel_id=1, source_target_pairs={{0,8},{8,16},{16,24},{24,32},{32,40},{40,48},{48,56},{56,64},{64,7... | collective-permute-start | bytes 1179656 | tf_op jit(solution)/shard_map/while/body/eval_jaxpr/ppermute | solution.py:17
  45.2 9.3 %collective-permute-start = (bf16[2,768,128]{2,1,0:T(8,128)(2,1)}, bf16[2,768,128]{2,1,0:T(8,128)(2,1)S(1)}, u32[]{:S(2)}, u32[]{:S(2)}) collective-permute-start(bf16[2,768,128]{2,1,0:T(8,128)(2,1)} %get-tuple-element.297), channel_id=1, source_target_pairs={{0,8},{8,16},{16,24},{24,32},{32,40},{40,48},{48,56},{56,64},{64,7... | collective-permute-start | bytes 1179656 | tf_op jit(solution)/shard_map/while/body/eval_jaxpr/ppermute | solution.py:17
  56.0 10.6 %collective-permute-start = (bf16[2,768,128]{2,1,0:T(8,128)(2,1)}, bf16[2,768,128]{2,1,0:T(8,128)(2,1)S(1)}, u32[]{:S(2)}, u32[]{:S(2)}) collective-permute-start(bf16[2,768,128]{2,1,0:T(8,128)(2,1)} %get-tuple-element.297), channel_id=1, source_target_pairs={{0,8},{8,16},{16,24},{24,32},{32,40},{40,48},{48,56},{56,64},{64,7... | collective-permute-start | bytes 1179656 | tf_op jit(solution)/shard_map/while/body/eval_jaxpr/ppermute | solution.py:17
  68.1 11.4 %collective-permute-start = (bf16[2,768,128]{2,1,0:T(8,128)(2,1)}, bf16[2,768,128]{2,1,0:T(8,128)(2,1)S(1)}, u32[]{:S(2)}, u32[]{:S(2)}) collective-permute-start(bf16[2,768,128]{2,1,0:T(8,128)(2,1)} %get-tuple-element.297), channel_id=1, source_target_pairs={{0,8},{8,16},{16,24},{24,32},{32,40},{40,48},{48,56},{56,64},{64,7... | collective-permute-start | bytes 1179656 | tf_op jit(solution)/shard_map/while/body/eval_jaxpr/ppermute | solution.py:17
  81.0 3.5 %copy-start.4 = (s32[6,16]{1,0:T(8,128)S(1)}, s32[6,16]{1,0:T(8,128)}, u32[]{:S(2)}) copy-start(s32[6,16]{1,0:T(8,128)} %param.16) | copy-start | bytes 1156
  81.0 3.5 %copy-start.6 = (s32[6]{0:T(128)S(1)}, s32[6]{0:T(128)}, u32[]{:S(2)}) copy-start(s32[6]{0:T(128)} %param.17) | copy-start | bytes 76
  84.5 45.4 %copy-start.7 = (bf16[128]{0:T(256)(128)(2,1)S(1)}, bf16[128]{0:T(256)(128)(2,1)}, u32[]{:S(2)}) copy-start(bf16[128]{0:T(256)(128)(2,1)} %param.14) | copy-start | bytes 772
  84.5 45.4 %copy-start.3 = (bf16[128,1024]{1,0:T(8,128)(2,1)S(1)}, bf16[128,1024]{1,0:T(8,128)(2,1)}, u32[]{:S(2)}) copy-start(bf16[128,1024]{1,0:T(8,128)(2,1)} %param.15) | copy-start | bytes 786436
Sparse Core Ops, SparseCore 0:
  133.3 71.8 reduce-scatter.1
where the time goes:
time: 215 us; the launch traced here: 214 us
  waiting for transfers between devices  95.9 us (45%)
  starting transfers between devices  35.3 us (16%)
  matrix products  27.7 us (13%)
  local copies, waits for them, and re-layouts  24.9 us (12%)
  between operations  13.5 us (6%)
  other arithmetic  12.1 us (6%)
  loops' own time  4.47 us (2%)
    reduce_scatter x1, waiting for transfers between devices, body(): lax.psum_scatter(partial_terms, 'head', scatter_dimension=1, tiled=True)  72 us
    ppermute x6, starting transfers between devices, shifted(): return lax.ppermute(shard, axis, pairs)  35.3 us
    ppermute x6, waiting for transfers between devices, shifted(): return lax.ppermute(shard, axis, pairs)  23.8 us
    dot_general x7, matrix products, visit(): jnp.einsum('hqk,khe->qhe', weights, visit_values, preferred_element_type=...  23.2 us
    while x13, local copies, waits for them, and re-layouts  6.5 us
    reshape x7, local copies, waits for them, and re-layouts, visit(): member_rows = member_rows.reshape(tok_rows, tok_rows)  4.77 us
    dynamic_update_slice x6, local copies, waits for them, and re-layouts, body(): last_one, earlier = lax.scan(advance, keys_values, None, length=reach_devs)  4.64 us
    another operation x1, loops' own time, body(): lax.scan(visit, start, (window, jnp.arange(depth, dtype=jnp.int32)))  4.41 us
  transfers between devices with their start and end apart: 7, of which 7 were waited for; matrix products, arithmetic and copies ran while one was open for 0% of the time, Pallas kernels for 0%

commit v1 on v0

v1 whole, which is shorter than its diff:
```python
import functools

import jax
import jax.numpy as jnp
from jax import lax
from jax.experimental import pallas as pl
from jax.experimental.pallas import tpu as pltpu
from jax.sharding import PartitionSpec as P

DH = 128
BLK = 128
EPS = 1e-05
MESH = pl.DeviceIdType.MESH
F32 = jnp.float32
BF16 = jnp.bfloat16
NT = (((1,), (1,)), ((), ()))


def silu(v):
    half = 0.5 * v
    return half + half * jnp.tanh(half)


def kernel(
    S, Y, NB,
    hist, lng, win, og, wout, lists, o_ref,
    xb, nb, wkv, wqg, wf, kv, sv, qb, gb, att, mr, gat, gall, ob,
    in_sem, w_sem, xs, xr, ps, pr, rs, rr, ls, lr, bs, br, cs, cr, a1s, a1r, a2s, a2r,
):
    tok = NB * BLK
    rows_peer = tok // Y
    s = lax.axis_index("seq")
    h = lax.axis_index("head")
    p = lax.rem(s, 2)
    nxt = lax.rem(s + 2, S)
    prv = lax.rem(s + S - 2, S)
    sib = s + 1 - 2 * p
    scale = 0.5 * DH ** (-0.5)

    def block_rows(i):
        return pl.ds(pl.multiple_of(i * BLK, BLK), BLK)

    def load_block(i):
        return pltpu.make_async_copy(hist.at[block_rows(i)], xb.at[block_rows(i)], in_sem.at[i])

    def load_w(which, dst, half, sem):
        return pltpu.make_async_copy(
            win.at[which], dst.at[:, pl.ds(half * DH, DH)], w_sem.at[sem]
        )

    loads = [load_w(3, wkv, 0, 0), load_w(1, wkv, 1, 1), load_w(2, wqg, 0, 2), load_w(0, wqg, 1, 3)]
    half_rows = DH // 2
    load_out = pltpu.make_async_copy(wout, wf.at[h], w_sem.at[4])
    load_block(NB - 1).start()
    loads[0].start()
    loads[1].start()
    for i in range(NB - 2, -1, -1):
        load_block(i).start()
    loads[2].start()
    loads[3].start()
    load_out.start()

    barrier = pltpu.get_barrier_semaphore()
    for who in (nxt, prv, sib):
        pl.semaphore_signal(barrier, inc=1, device_id={"seq": who}, device_id_type=MESH)
    for k in range(1, Y):
        pl.semaphore_signal(
            barrier, inc=1, device_id={"head": lax.rem(h + k, Y)}, device_id_type=MESH
        )

    def hop(l, i):
        return pltpu.make_async_remote_copy(
            src_ref=kv.at[l, i], dst_ref=kv.at[l + 1, i],
            send_sem=xs.at[l, i], recv_sem=xr.at[l, i],
            device_id={"seq": nxt}, device_id_type=MESH,
        )

    def push(k, i):
        return pltpu.make_async_remote_copy(
            src_ref=kv.at[k + p, i], dst_ref=sv.at[k, i],
            send_sem=ps.at[k, i], recv_sem=pr.at[k, i],
            device_id={"seq": sib}, device_id_type=MESH,
        )

    up = lax.rem(h + 1, Y)
    down = lax.rem(h + Y - 1, Y)

    def ring_up(r):
        at = lax.rem(h - r + 1 + Y, Y)
        return pltpu.make_async_remote_copy(
            src_ref=wf.at[at, p], dst_ref=wf.at[at, p],
            send_sem=rs.at[r], recv_sem=rr.at[r],
            device_id={"head": up}, device_id_type=MESH,
        )

    def ring_down(r):
        at = lax.rem(h + r - 1, Y)
        return pltpu.make_async_remote_copy(
            src_ref=wf.at[at, p], dst_ref=wf.at[at, p],
            send_sem=ls.at[r], recv_sem=lr.at[r],
            device_id={"head": down}, device_id_type=MESH,
        )

    def share_up(r, half):
        at = lax.rem(h - r + Y, Y)
        return pltpu.make_async_remote_copy(
            src_ref=wf.at[at, half], dst_ref=wf.at[at, half],
            send_sem=bs.at[r], recv_sem=br.at[r],
            device_id={"seq": sib}, device_id_type=MESH,
        )

    def share_down(r, half):
        at = lax.rem(h + r, Y)
        return pltpu.make_async_remote_copy(
            src_ref=wf.at[at, half], dst_ref=wf.at[at, half],
            send_sem=cs.at[r], recv_sem=cr.at[r],
            device_id={"seq": sib}, device_id_type=MESH,
        )

    n_up = Y // 2
    n_down = Y - 1 - n_up

    def ring_step(n):
        @pl.when((n >= 1) & (n <= n_up))
        def _():
            ring_up(n).wait_recv()
            share_up(n, p).start()

        @pl.when((n >= 1) & (n <= n_down))
        def _():
            ring_down(n).wait_recv()
            share_down(n, p).start()

        @pl.when(n + 1 <= n_up)
        def _():
            ring_up(n + 1).start()

        @pl.when(n + 1 <= n_down)
        def _():
            ring_down(n + 1).start()

    loads[0].wait()
    loads[1].wait()
    gain = lng[...].astype(F32)

    def project(n, carry):
        i = NB - 1 - n
        load_block(i).wait()
        for piece in range(4):
            at = pl.ds(pl.multiple_of(i * BLK + piece * 32, 32), 32)
            floats = xb[at, :].astype(F32)
            centred = floats - jnp.mean(floats, axis=-1, keepdims=True)
            spread = jnp.mean(centred * centred, axis=-1, keepdims=True)
            nb[at, :] = (centred * lax.rsqrt(spread + EPS) * gain).astype(BF16)
        both = silu(jnp.dot(nb[block_rows(i), :], wkv[...], preferred_element_type=F32)).astype(BF16)
        kv[0, i, 0] = both[:, :DH]
        kv[0, i, 1] = both[:, DH:]

        @pl.when(n == 0)
        def _():
            pl.semaphore_wait(barrier, 3 + Y - 1)

        hop(0, i).start()

        @pl.when(p == 0)
        def _():
            push(0, i).start()

        return carry

    lax.fori_loop(0, NB, project, 0)
    load_out.wait()
    ring_step(0)

    loads[2].wait()
    loads[3].wait()

    def project_q(i, carry):
        both = silu(jnp.dot(nb[block_rows(i), :], wqg[...], preferred_element_type=F32)).astype(BF16)
        qb[block_rows(i), :] = both[:, :DH]
        gb[block_rows(i), :] = both[:, DH:]
        return carry

    lax.fori_loop(0, NB, project_q, 0)

    shape = mr.shape[1:]
    row = lax.broadcasted_iota(jnp.int32, shape, 0)
    lane = lax.broadcasted_iota(jnp.int32, shape, 1)
    back = (row * 11) >> 5
    key_id = NB * (s - back) + 2 * (row - 3 * back) + (lane >> 7)
    for j in range(NB):
        listed = key_id == lists[j, 0]
        for k in range(1, lists.shape[1]):
            listed = listed | (key_id == lists[j, k])
        mr[j] = jnp.where(listed, 1.0, 0.0)

    def attend(keys, values, at, first, t_own):
        m = (NB - first) * BLK
        scores = lax.dot_general(qb[first * BLK :, :], keys, NT, preferred_element_type=F32)
        pieces = []
        for j in range(first, NB):
            half = scores[(j - first) * BLK : (j - first + 1) * BLK] * scale
            keep = mr[j, pl.ds(at, 1), :]
            kept = half * keep
            weight = kept + kept * jnp.tanh(half)
            if t_own is not None and j <= 2 * t_own + 1:
                q_at = j * BLK + lax.broadcasted_iota(jnp.int32, weight.shape, 0)
                k_at = 2 * t_own * BLK + lax.broadcasted_iota(jnp.int32, weight.shape, 1)
                weight = jnp.where(k_at <= q_at, weight, 0.0)
            pieces.append(weight.astype(BF16))
        weights = jnp.concatenate(pieces, axis=0)
        update = jnp.dot(weights, values, preferred_element_type=F32)
        if t_own == 0:
            att[...] = update
        else:
            att[first * BLK :, :] += update

    def pair(buf, l, t):
        blocks = pl.ds(2 * t, 2)
        return buf[l, blocks, 0].reshape(2 * BLK, DH), buf[l, blocks, 1].reshape(2 * BLK, DH)

    for t in range(NB // 2):
        keys, values = pair(kv, 0, t)
        attend(keys, values, t, 2 * t, t)

    def middle(n, carry):
        l = 1 + n // 3
        t = 2 - lax.rem(n, 3)
        for i in (2 * t + 1, 2 * t):
            hop(l - 1, i).wait_recv()

            @pl.when((l == 1) | (p == 1) | (i == NB - 1))
            def _():
                hop(l, i).start()

            push(l - p, i).start()
        ring_step(n + 1)
        keys, values = pair(kv, l, t)
        attend(keys, values, 3 * (2 * l) + t, 0, None)
        for i in (2 * t + 1, 2 * t):
            push(l - 1, i).wait_recv()
        keys, values = pair(sv, l - 1, t)
        attend(keys, values, 3 * (2 * l - 1) + t, 0, None)
        return carry

    lax.fori_loop(0, 6, middle, 0)

    def last(n, carry):
        t = 2 - n
        for i in (2 * t + 1, 2 * t):

            @pl.when((p == 1) | (i == NB - 1))
            def _():
                hop(2, i).wait_recv()

            @pl.when(p == 1)
            def _():
                push(2, i).start()

        for i in (2 * t + 1, 2 * t):
            push(2, i).wait_recv()
        keys, values = pair(sv, 2, t)
        attend(keys, values, 3 * 5 + t, 0, None)
        return carry

    lax.fori_loop(0, 3, last, 0)

    scores = lax.dot_general(qb[:BLK, :], kv[3, NB - 1, 0], NT, preferred_element_type=F32)
    half = scores * scale
    kept = half * mr[0, 3 * 6 + 2 : 3 * 6 + 3, BLK:]
    weight = (kept + kept * jnp.tanh(half)).astype(BF16)
    att[:BLK, :] += jnp.dot(weight, kv[3, NB - 1, 1], preferred_element_type=F32)

    out_gain = og[...].astype(F32)
    for j in range(NB):
        at = slice(j * BLK, (j + 1) * BLK)
        floats = att[at, :]
        centred = floats - jnp.mean(floats, axis=-1, keepdims=True)
        spread = jnp.mean(centred * centred, axis=-1, keepdims=True)
        gat[at, :] = (
            centred * lax.rsqrt(spread + EPS) * out_gain * gb[at, :].astype(F32)
        ).astype(BF16)

    def share_rows(y):
        return pl.ds(pl.multiple_of(y * rows_peer, 32), rows_peer)

    def to_rows(k):
        peer = lax.rem(h + k, Y)
        return pltpu.make_async_remote_copy(
            src_ref=gat.at[share_rows(peer)], dst_ref=gall.at[h],
            send_sem=a1s.at[k], recv_sem=a1r.at[k],
            device_id={"head": peer}, device_id_type=MESH,
        )

    def to_columns(k):
        peer = lax.rem(h + k, Y)
        return pltpu.make_async_remote_copy(
            src_ref=ob.at[peer], dst_ref=o_ref.at[share_rows(h)],
            send_sem=a2s.at[k], recv_sem=a2r.at[k],
            device_id={"head": peer}, device_id_type=MESH,
        )

    for k in range(1, Y):
        to_rows(k).start()
    gall[h] = gat[share_rows(h), :]
    for r in range(1, n_up + 1):
        share_up(r, 1 - p).wait_recv()
    for r in range(1, n_down + 1):
        share_down(r, 1 - p).wait_recv()
    for k in range(1, Y):
        to_rows(k).wait_recv()
    gated = jnp.concatenate([gall[y] for y in range(Y)], axis=1)
    cols = ob.shape[2]
    for y in range(Y):
        at = slice(y * cols, (y + 1) * cols)
        weights = wf[:, :, :, at].reshape(Y * DH, cols)
        summed = jnp.dot(gated, weights, preferred_element_type=F32)
        ob[y] = (summed + xb[share_rows(h), at].astype(F32)).astype(BF16)
    for k in range(1, Y):
        to_columns(k).start()
    o_ref[share_rows(h), :] = ob[h]

    for l in range(2):
        for i in range(NB):
            hop(l, i).wait_send()
    for k in range(3):
        for i in range(NB):
            push(k, i).wait_send()
    hop(2, NB - 1).wait_send()

    @pl.when(p == 1)
    def _():
        for i in range(NB - 1):
            hop(2, i).wait_send()

    for r in range(1, n_up + 1):
        ring_up(r).wait_send()
        share_up(r, p).wait_send()
    for r in range(1, n_down + 1):
        ring_down(r).wait_send()
        share_down(r, p).wait_send()
    for k in range(1, Y):
        to_rows(k).wait_send()
        to_columns(k).wait_send()
        to_columns(k).wait_recv()


def solution(mesh):
    S, Y = mesh.shape["seq"], mesh.shape["head"]

    def body(history, ln_gain, w_in, out_gain, w_out, block_lists, counts):
        tok, width = history.shape
        NB = tok // BLK
        cols = width // Y
        vmem = pl.BlockSpec(memory_space=pltpu.VMEM)
        hbm = pl.BlockSpec(memory_space=pl.ANY)
        dma = pltpu.SemaphoreType.DMA
        return pl.pallas_call(
            functools.partial(kernel, S, Y, NB),
            out_shape=jax.ShapeDtypeStruct((tok, cols), BF16),
            in_specs=[hbm, vmem, hbm, vmem, hbm, pl.BlockSpec(memory_space=pltpu.SMEM)],
            out_specs=vmem,
            scratch_shapes=[
                pltpu.VMEM((tok, width), BF16),
                pltpu.VMEM((tok, width), BF16),
                pltpu.VMEM((width, 2 * DH), BF16),
                pltpu.VMEM((width, 2 * DH), BF16),
                pltpu.VMEM((Y, 2, DH // 2, width), BF16),
                pltpu.VMEM((4, NB, 2, BLK, DH), BF16),
                pltpu.VMEM((3, NB, 2, BLK, DH), BF16),
                pltpu.VMEM((tok, DH), BF16),
                pltpu.VMEM((tok, DH), BF16),
                pltpu.VMEM((tok, DH), F32),
                pltpu.VMEM((NB, 24, 2 * BLK), F32),
                pltpu.VMEM((tok, DH), BF16),
                pltpu.VMEM((Y, tok // Y, DH), BF16),
                pltpu.VMEM((Y, tok // Y, cols), BF16),
                dma((NB,)), dma((5,)),
                dma((3, NB)), dma((3, NB)), dma((3, NB)), dma((3, NB)),
                dma((Y,)), dma((Y,)), dma((Y,)), dma((Y,)),
                dma((Y,)), dma((Y,)), dma((Y,)), dma((Y,)),
                dma((Y,)), dma((Y,)), dma((Y,)), dma((Y,)),
            ],
            compiler_params=pltpu.CompilerParams(
                collective_id=0, has_side_effects=True, vmem_limit_bytes=56 * 2**20
            ),
        )(
            history, ln_gain.reshape(1, width), w_in, out_gain.reshape(1, DH),
            w_out.reshape(2, DH // 2, width), block_lists,
        )

    placed = (
        P("seq", None),
        P(),
        P(None, None, "head"),
        P("head"),
        P("head", None),
        P("seq", None),
        P("seq"),
    )
    return jax.shard_map(
        body, mesh=mesh, in_specs=placed, out_specs=P("seq", "head"), check_vma=False
    )
```

time: 215 us -> 68 us (0.32)
  the two profiles are of different devices: /device:TPU:14 before, /device:TPU:2 now
where the time goes in v1:
time: 68 us; the launch traced here: 67.7 us
  Pallas kernels  64.8 us (95%)
  local copies, waits for them, and re-layouts  2.89 us (4%)
    pallas_call x1, Pallas kernels, body(): pl.pallas_call(functools.partial(kernel, S, Y, NB), out_shape=jax.ShapeDt...  64.8 us
    unnamed x1, local copies, waits for them, and re-layouts  1.62 us

profile of v1, /device:TPU:2, one launch (start us, length us, event | category | flops | bytes accessed | tf_op | source)
XLA Modules:
  0.0 67.7 jit_solution(10612927020100230988)
XLA Ops:
  0.0 1.3 %reshape.9.lng = bf16[1,1024]{1,0:T(2,128)(2,1)} reshape(bf16[1024]{0:T(1024)(128)(2,1)} %param.8) | data formatting | bytes 4096 | tf_op jit(solution)/shard_map/reshape | solution.py:388
  1.3 64.8 %shard_map.64 = bf16[768,128]{1,0:T(8,128)(2,1)} custom-call(bf16[768,1024]{1,0:T(8,128)(2,1)} %hist.1, bf16[1,1024]{1,0:T(2,128)(2,1)} %reshape.9.lng, bf16[4,1024,128]{2,1,0:T(8,128)(2,1)} %win.1, bf16[1,128]{1,0:T(2,128)(2,1)} %bitcast.3, bf16[2,64,1024]{2,1,0:T(8,128)(2,1)} %bitcast.2, s32[6,16]{1,0:T(8,128)} %lists.1), custom_call_target="tpu_custom_call" | custom-call | tf_op jit(solution)/shard_map/pallas_call | solution.py:358
  66.1 1.6 %copy.8 = bf16[768,128]{1,0:T(8,128)(2,1)} copy(bf16[768,128]{1,0:T(8,128)(2,1)} %shard_map.64) | data formatting | bytes 393216

commit v2 on v1

--- a/solution.py
+++ b/solution.py
@@ -27,13 +27,14 @@
     xb, nb, wkv, wqg, wf, kv, sv, qb, gb, att, mr, gat, gall, ob,
     in_sem, w_sem, xs, xr, ps, pr, rs, rr, ls, lr, bs, br, cs, cr, a1s, a1r, a2s, a2r,
 ):
-    tok = NB * BLK
-    rows_peer = tok // Y
+    share = BLK // Y
     s = lax.axis_index("seq")
     h = lax.axis_index("head")
     p = lax.rem(s, 2)
-    nxt = lax.rem(s + 2, S)
-    prv = lax.rem(s + S - 2, S)
+    chip = lax.div(s, 2)
+    is_first, is_last = chip == 0, chip == S // 2 - 1
+    nxt = jnp.minimum(s + 2, S - 1)
+    prv = jnp.maximum(s - 2, 0)
     sib = s + 1 - 2 * p
     scale = 0.5 * DH ** (-0.5)
 
@@ -61,8 +62,16 @@
     load_out.start()
 
     barrier = pltpu.get_barrier_semaphore()
-    for who in (nxt, prv, sib):
-        pl.semaphore_signal(barrier, inc=1, device_id={"seq": who}, device_id_type=MESH)
+    pl.semaphore_signal(barrier, inc=1, device_id={"seq": sib}, device_id_type=MESH)
+
+    @pl.when(~is_last)
+    def _():
+        pl.semaphore_signal(barrier, inc=1, device_id={"seq": nxt}, device_id_type=MESH)
+
+    @pl.when(~is_first)
+    def _():
+        pl.semaphore_signal(barrier, inc=1, device_id={"seq": prv}, device_id_type=MESH)
+
     for k in range(1, Y):
         pl.semaphore_signal(
             barrier, inc=1, device_id={"head": lax.rem(h + k, Y)}, device_id_type=MESH
@@ -141,7 +150,7 @@
 
     loads[0].wait()
     loads[1].wait()
-    gain = lng[...].astype(F32)
+    gain = lng[...].astype(F32).reshape(1, -1)
 
     def project(n, carry):
         i = NB - 1 - n
@@ -158,9 +167,11 @@
 
         @pl.when(n == 0)
         def _():
-            pl.semaphore_wait(barrier, 3 + Y - 1)
-
-        hop(0, i).start()
+            pl.semaphore_wait(barrier, Y + (chip > 0).astype(jnp.int32) + (chip < S // 2 - 1).astype(jnp.int32))
+
+        @pl.when(~is_last)
+        def _():
+            hop(0, i).start()
 
         @pl.when(p == 0)
         def _():
@@ -223,115 +234,168 @@
         keys, values = pair(kv, 0, t)
         attend(keys, values, t, 2 * t, t)
 
+    def has_lane(l):
+        return chip >= l
+
+    def has_shared(k):
+        return chip + p >= k + 1
+
     def middle(n, carry):
         l = 1 + n // 3
         t = 2 - lax.rem(n, 3)
-        for i in (2 * t + 1, 2 * t):
-            hop(l - 1, i).wait_recv()
-
-            @pl.when((l == 1) | (p == 1) | (i == NB - 1))
-            def _():
-                hop(l, i).start()
-
-            push(l - p, i).start()
+
+        @pl.when(has_lane(l))
+        def _():
+            for i in (2 * t + 1, 2 * t):
+                hop(l - 1, i).wait_recv()
+
+                @pl.when(((l == 1) | (p == 1) | (i == NB - 1)) & ~is_last)
+                def _():
+                    hop(l, i).start()
+
+                push(l - p, i).start()
+
         ring_step(n + 1)
-        keys, values = pair(kv, l, t)
-        attend(keys, values, 3 * (2 * l) + t, 0, None)
-        for i in (2 * t + 1, 2 * t):
-            push(l - 1, i).wait_recv()
-        keys, values = pair(sv, l - 1, t)
-        attend(keys, values, 3 * (2 * l - 1) + t, 0, None)
+
+        @pl.when(has_lane(l))
+        def _():
+            keys, values = pair(kv, l, t)
+            attend(keys, values, 3 * (2 * l) + t, 0, None)
+
+        @pl.when(has_shared(l - 1))
+        def _():
+            for i in (2 * t + 1, 2 * t):
+                push(l - 1, i).wait_recv()
+            keys, values = pair(sv, l - 1, t)
+            attend(keys, values, 3 * (2 * l - 1) + t, 0, None)
+
         return carry
 
     lax.fori_loop(0, 6, middle, 0)
 
-    def last(n, carry):
-        t = 2 - n
-        for i in (2 * t + 1, 2 * t):
-
-            @pl.when((p == 1) | (i == NB - 1))
-            def _():
-                hop(2, i).wait_recv()
-
-            @pl.when(p == 1)
-            def _():
-                push(2, i).start()
-
-        for i in (2 * t + 1, 2 * t):
-            push(2, i).wait_recv()
-        keys, values = pair(sv, 2, t)
-        attend(keys, values, 3 * 5 + t, 0, None)
-        return carry
-
-    lax.fori_loop(0, 3, last, 0)
-
-    scores = lax.dot_general(qb[:BLK, :], kv[3, NB - 1, 0], NT, preferred_element_type=F32)
-    half = scores * scale
-    kept = half * mr[0, 3 * 6 + 2 : 3 * 6 + 3, BLK:]
-    weight = (kept + kept * jnp.tanh(half)).astype(BF16)
-    att[:BLK, :] += jnp.dot(weight, kv[3, NB - 1, 1], preferred_element_type=F32)
-
-    out_gain = og[...].astype(F32)
-    for j in range(NB):
-        at = slice(j * BLK, (j + 1) * BLK)
-        floats = att[at, :]
-        centred = floats - jnp.mean(floats, axis=-1, keepdims=True)
-        spread = jnp.mean(centred * centred, axis=-1, keepdims=True)
-        gat[at, :] = (
-            centred * lax.rsqrt(spread + EPS) * out_gain * gb[at, :].astype(F32)
-        ).astype(BF16)
-
-    def share_rows(y):
-        return pl.ds(pl.multiple_of(y * rows_peer, 32), rows_peer)
-
-    def to_rows(k):
+    def take_third(i):
+        @pl.when(has_lane(3) & (p == 1))
+        def _():
+            hop(2, i).wait_recv()
+            push(2, i).start()
+
+    def attend_shared(t):
+        @pl.when(has_shared(2))
+        def _():
+            for i in (2 * t + 1, 2 * t):
+                push(2, i).wait_recv()
+            keys, values = pair(sv, 2, t)
+            attend(keys, values, 3 * 5 + t, 0, None)
+
+    half_blocks = NB // 2
+
+    def some(part):
+        return pl.ds(part * half_blocks, half_blocks)
+
+    def to_rows(part, k):
         peer = lax.rem(h + k, Y)
         return pltpu.make_async_remote_copy(
-            src_ref=gat.at[share_rows(peer)], dst_ref=gall.at[h],
-            send_sem=a1s.at[k], recv_sem=a1r.at[k],
+            src_ref=gat.at[some(part), peer], dst_ref=gall.at[h, some(part)],
+            send_sem=a1s.at[part, k], recv_sem=a1r.at[part, k],
             device_id={"head": peer}, device_id_type=MESH,
         )
 
-    def to_columns(k):
+    def to_columns(part, k):
         peer = lax.rem(h + k, Y)
         return pltpu.make_async_remote_copy(
-            src_ref=ob.at[peer], dst_ref=o_ref.at[share_rows(h)],
-            send_sem=a2s.at[k], recv_sem=a2r.at[k],
+            src_ref=ob.at[peer, some(part)], dst_ref=o_ref.at[some(part), h],
+            send_sem=a2s.at[part, k], recv_sem=a2r.at[part, k],
             device_id={"head": peer}, device_id_type=MESH,
         )
 
-    for k in range(1, Y):
-        to_rows(k).start()
-    gall[h] = gat[share_rows(h), :]
+    def keep_columns(part):
+        return pltpu.make_async_copy(ob.at[h, some(part)], o_ref.at[some(part), h], a2r.at[part, 0])
+
+    far_first = sorted(range(1, Y), key=lambda k: -min(k, Y - k))
+    out_gain = og[...].astype(F32).reshape(1, -1)
+
+    def finish(part):
+        for j in range(part * half_blocks, (part + 1) * half_blocks):
+            at = slice(j * BLK, (j + 1) * BLK)
+            floats = att[at, :]
+            centred = floats - jnp.mean(floats, axis=-1, keepdims=True)
+            spread = jnp.mean(centred * centred, axis=-1, keepdims=True)
+            normed = centred * lax.rsqrt(spread + EPS) * out_gain * gb[at, :].astype(F32)
+            gat[j] = normed.astype(BF16).reshape(Y, share, DH)
+        for k in far_first:
+            to_rows(part, k).start()
+        gall[h, some(part)] = gat[some(part), h]
+
+    def mix(part):
+        for k in far_first:
+            to_rows(part, k).wait_recv()
+        rows = half_blocks * share
+        gated = jnp.concatenate(
+            [gall[y, some(part)].reshape(rows, DH) for y in range(Y)], axis=1
+        )
+        cols = ob.shape[3]
+        for y in range(Y):
+            at = slice(y * cols, (y + 1) * cols)
+            weights = wf[:, :, :, at].reshape(Y * DH, cols)
+            summed = jnp.dot(gated, weights, preferred_element_type=F32)
+            for n in range(half_blocks):
+                j = part * half_blocks + n
+                mine = pl.ds(pl.multiple_of(j * BLK + h * share, share), share)
+                ob[y, j] = (
+                    summed[n * share : (n + 1) * share] + xb[mine, at].astype(F32)
+                ).astype(BF16)
+        for k in far_first:
+            to_columns(part, k).start()
+        keep_columns(part).start()
+
+    take_third(5)
+    attend_shared(2)
+    take_third(4)
+    attend_shared(1)
+    finish(1)
+    take_third(3)
+    take_third(2)
+    attend_shared(0)
+
+    @pl.when(has_lane(3))
+    def _():
+        @pl.when(p == 0)
+        def _():
+            hop(2, NB - 1).wait_recv()
+
+        scores = lax.dot_general(qb[:BLK, :], kv[3, NB - 1, 0], NT, preferred_element_type=F32)
+        half = scores * scale
+        kept = half * mr[0, 3 * 6 + 2 : 3 * 6 + 3, BLK:]
+        weight = (kept + kept * jnp.tanh(half)).astype(BF16)
+        att[:BLK, :] += jnp.dot(weight, kv[3, NB - 1, 1], preferred_element_type=F32)
+
+    finish(0)
+    take_third(1)
+    take_third(0)
     for r in range(1, n_up + 1):
         share_up(r, 1 - p).wait_recv()
     for r in range(1, n_down + 1):
         share_down(r, 1 - p).wait_recv()
-    for k in range(1, Y):
-        to_rows(k).wait_recv()
-    gated = jnp.concatenate([gall[y] for y in range(Y)], axis=1)
-    cols = ob.shape[2]
-    for y in range(Y):
-        at = slice(y * cols, (y + 1) * cols)
-        weights = wf[:, :, :, at].reshape(Y * DH, cols)
-        summed = jnp.dot(gated, weights, preferred_element_type=F32)
-        ob[y] = (summed + xb[share_rows(h), at].astype(F32)).astype(BF16)
-    for k in range(1, Y):
-        to_columns(k).start()
-    o_ref[share_rows(h), :] = ob[h]
-
-    for l in range(2):
-        for i in range(NB):
-            hop(l, i).wait_send()
-    for k in range(3):
-        for i in range(NB):
-            push(k, i).wait_send()
-    hop(2, NB - 1).wait_send()
-
-    @pl.when(p == 1)
-    def _():
-        for i in range(NB - 1):
-            hop(2, i).wait_send()
+    mix(1)
+    mix(0)
+
+    for l in range(3):
+
+        @pl.when(has_lane(l) & ~is_last)
+        def _():
+            for i in range(NB):
+                if l < 2 or i == NB - 1:
+                    hop(l, i).wait_send()
+                else:
+
+                    @pl.when(p == 1)
+                    def _():
+                        hop(l, i).wait_send()
+
+        @pl.when(has_lane(l + p))
+        def _():
+            for i in range(NB):
+                push(l, i).wait_send()
 
     for r in range(1, n_up + 1):
         ring_up(r).wait_send()
@@ -339,10 +403,12 @@
     for r in range(1, n_down + 1):
         ring_down(r).wait_send()
         share_down(r, p).wait_send()
-    for k in range(1, Y):
-        to_rows(k).wait_send()
-        to_columns(k).wait_send()
-        to_columns(k).wait_recv()
+    for part in range(2):
+        keep_columns(part).wait()
+        for k in range(1, Y):
+            to_rows(part, k).wait_send()
+            to_columns(part, k).wait_send()
+            to_columns(part, k).wait_recv()
 
 
 def solution(mesh):
@@ -353,13 +419,13 @@
         NB = tok // BLK
         cols = width // Y
         vmem = pl.BlockSpec(memory_space=pltpu.VMEM)
-        hbm = pl.BlockSpec(memory_space=pl.ANY)
+        hbm = pl.BlockSpec(memory_space=pltpu.HBM)
         dma = pltpu.SemaphoreType.DMA
         return pl.pallas_call(
             functools.partial(kernel, S, Y, NB),
-            out_shape=jax.ShapeDtypeStruct((tok, cols), BF16),
+            out_shape=jax.ShapeDtypeStruct((NB, Y, BLK // Y, cols), BF16),
             in_specs=[hbm, vmem, hbm, vmem, hbm, pl.BlockSpec(memory_space=pltpu.SMEM)],
-            out_specs=vmem,
+            out_specs=hbm,
             scratch_shapes=[
                 pltpu.VMEM((tok, width), BF16),
                 pltpu.VMEM((tok, width), BF16),
@@ -372,22 +438,22 @@
                 pltpu.VMEM((tok, DH), BF16),
                 pltpu.VMEM((tok, DH), F32),
                 pltpu.VMEM((NB, 24, 2 * BLK), F32),
-                pltpu.VMEM((tok, DH), BF16),
-                pltpu.VMEM((Y, tok // Y, DH), BF16),
-                pltpu.VMEM((Y, tok // Y, cols), BF16),
+                pltpu.VMEM((NB, Y, BLK // Y, DH), BF16),
+                pltpu.VMEM((Y, NB, BLK // Y, DH), BF16),
+                pltpu.VMEM((Y, NB, BLK // Y, cols), BF16),
                 dma((NB,)), dma((5,)),
                 dma((3, NB)), dma((3, NB)), dma((3, NB)), dma((3, NB)),
                 dma((Y,)), dma((Y,)), dma((Y,)), dma((Y,)),
                 dma((Y,)), dma((Y,)), dma((Y,)), dma((Y,)),
-                dma((Y,)), dma((Y,)), dma((Y,)), dma((Y,)),
+                dma((2, Y)), dma((2, Y)), dma((2, Y)), dma((2, Y)),
             ],
             compiler_params=pltpu.CompilerParams(
                 collective_id=0, has_side_effects=True, vmem_limit_bytes=56 * 2**20
             ),
         )(
-            history, ln_gain.reshape(1, width), w_in, out_gain.reshape(1, DH),
+            history, ln_gain, w_in, out_gain,
             w_out.reshape(2, DH // 2, width), block_lists,
-        )
+        ).reshape(tok, cols)
 
     placed = (
         P("seq", None),

time: 68 us -> 54.8 us (0.81)
  the two profiles are of different devices: /device:TPU:2 before, /device:TPU:16 now
where the time goes in v2:
time: 54.8 us; the launch traced here: 54.6 us
  Pallas kernels  53 us (97%)
  local copies, waits for them, and re-layouts  1.62 us (3%)
    pallas_call x1, Pallas kernels, body(): pl.pallas_call(functools.partial(kernel, S, Y, NB), out_shape=jax.ShapeDt...  53 us
    unnamed x1, local copies, waits for them, and re-layouts  1.62 us

profile of v2, /device:TPU:16, one launch (start us, length us, event | category | flops | bytes accessed | tf_op | source)
XLA Modules:
  0.0 54.6 jit_solution(7867199985517120246)
XLA Ops:
  0.0 53.0 %shard_map.64 = bf16[6,8,16,128]{3,2,1,0:T(8,128)(2,1)} custom-call(bf16[768,1024]{1,0:T(8,128)(2,1)} %hist.1, bf16[1024]{0:T(1024)(128)(2,1)} %lng.1, bf16[4,1024,128]{2,1,0:T(8,128)(2,1)} %win.1, bf16[128]{0:T(256)(128)(2,1)} %og.1, bf16[2,64,1024]{2,1,0:T(8,128)(2,1)} %bitcast.3, s32[6,16]{1,0:T(8,128)} %lists.1), custom_call_target="tpu_custom_call" | custom-call | tf_op jit(solution)/shard_map/pallas_call | solution.py:424
  53.0 1.6 %copy.8 = bf16[768,128]{1,0:T(8,128)(2,1)} copy(bf16[768,128]{1,0:T(8,128)(2,1)} %bitcast.2) | data formatting | bytes 393216

commit v3 on v2

--- a/solution.py
+++ b/solution.py
@@ -25,7 +25,7 @@
     S, Y, NB,
     hist, lng, win, og, wout, lists, o_ref,
     xb, nb, wkv, wqg, wf, kv, sv, qb, gb, att, mr, gat, gall, ob,
-    in_sem, w_sem, xs, xr, ps, pr, rs, rr, ls, lr, bs, br, cs, cr, a1s, a1r, a2s, a2r,
+    in_sem, w_sem, xs, xr, ps, pr, rs, rr, ls, lr, bs, br, cs, cr, a1s, a1r, a2s, a2r, fs,
 ):
     share = BLK // Y
     s = lax.axis_index("seq")
@@ -55,23 +55,25 @@
     load_block(NB - 1).start()
     loads[0].start()
     loads[1].start()
+    load_out.start()
     for i in range(NB - 2, -1, -1):
         load_block(i).start()
     loads[2].start()
     loads[3].start()
-    load_out.start()
 
     barrier = pltpu.get_barrier_semaphore()
     pl.semaphore_signal(barrier, inc=1, device_id={"seq": sib}, device_id_type=MESH)
-
-    @pl.when(~is_last)
-    def _():
-        pl.semaphore_signal(barrier, inc=1, device_id={"seq": nxt}, device_id_type=MESH)
 
     @pl.when(~is_first)
     def _():
         pl.semaphore_signal(barrier, inc=1, device_id={"seq": prv}, device_id_type=MESH)
 
+    @pl.when(~is_first & (p == 0))
+    def _():
+        pl.semaphore_signal(
+            barrier, inc=1, device_id={"seq": jnp.maximum(s - 1, 0)}, device_id_type=MESH
+        )
+
     for k in range(1, Y):
         pl.semaphore_signal(
             barrier, inc=1, device_id={"head": lax.rem(h + k, Y)}, device_id_type=MESH
@@ -90,6 +92,19 @@
             send_sem=ps.at[k, i], recv_sem=pr.at[k, i],
             device_id={"seq": sib}, device_id_type=MESH,
         )
+
+    def third(i):
+        return pltpu.make_async_remote_copy(
+            src_ref=kv.at[2, i], dst_ref=sv.at[2, i],
+            send_sem=xs.at[2, i], recv_sem=pr.at[2, i],
+            device_id={"seq": jnp.minimum(s + 1, S - 1)}, device_id_type=MESH,
+        )
+
+    third_shared = pltpu.make_async_remote_copy(
+        src_ref=sv.at[2, NB - 1], dst_ref=kv.at[3, NB - 1],
+        send_sem=fs.at[0], recv_sem=xr.at[2, NB - 1],
+        device_id={"seq": sib}, device_id_type=MESH,
+    )
 
     up = lax.rem(h + 1, Y)
     down = lax.rem(h + Y - 1, Y)
@@ -167,7 +182,7 @@
 
         @pl.when(n == 0)
         def _():
-            pl.semaphore_wait(barrier, Y + (chip > 0).astype(jnp.int32) + (chip < S // 2 - 1).astype(jnp.int32))
+            pl.semaphore_wait(barrier, Y + (chip < S // 2 - 1).astype(jnp.int32) * (1 + p))
 
         @pl.when(~is_last)
         def _():
@@ -177,11 +192,14 @@
         def _():
             push(0, i).start()
 
+        @pl.when(n == 0)
+        def _():
+            load_out.wait()
+            ring_step(0)
+
         return carry
 
     lax.fori_loop(0, NB, project, 0)
-    load_out.wait()
-    ring_step(0)
 
     loads[2].wait()
     loads[3].wait()
@@ -206,7 +224,6 @@
         mr[j] = jnp.where(listed, 1.0, 0.0)
 
     def attend(keys, values, at, first, t_own):
-        m = (NB - first) * BLK
         scores = lax.dot_general(qb[first * BLK :, :], keys, NT, preferred_element_type=F32)
         pieces = []
         for j in range(first, NB):
@@ -249,13 +266,16 @@
             for i in (2 * t + 1, 2 * t):
                 hop(l - 1, i).wait_recv()
 
-                @pl.when(((l == 1) | (p == 1) | (i == NB - 1)) & ~is_last)
+                @pl.when(((l == 1) | ((p == 0) & (i == NB - 1))) & ~is_last)
                 def _():
                     hop(l, i).start()
 
+                @pl.when((l == 2) & (p == 1) & ~is_last)
+                def _():
+                    third(i).start()
+
                 push(l - p, i).start()
 
-        ring_step(n + 1)
 
         @pl.when(has_lane(l))
         def _():
@@ -269,21 +289,25 @@
             keys, values = pair(sv, l - 1, t)
             attend(keys, values, 3 * (2 * l - 1) + t, 0, None)
 
+        @pl.when(lax.rem(n, 2) == 1)
+        def _():
+            ring_step((n + 1) // 2)
+
         return carry
 
     lax.fori_loop(0, 6, middle, 0)
-
-    def take_third(i):
-        @pl.when(has_lane(3) & (p == 1))
-        def _():
-            hop(2, i).wait_recv()
-            push(2, i).start()
 
     def attend_shared(t):
         @pl.when(has_shared(2))
         def _():
             for i in (2 * t + 1, 2 * t):
                 push(2, i).wait_recv()
+                if i == NB - 1:
+
+                    @pl.when(p == 0)
+                    def _():
+                        third_shared.start()
+
             keys, values = pair(sv, 2, t)
             attend(keys, values, 3 * 5 + t, 0, None)
 
@@ -348,21 +372,15 @@
             to_columns(part, k).start()
         keep_columns(part).start()
 
-    take_third(5)
     attend_shared(2)
-    take_third(4)
     attend_shared(1)
     finish(1)
-    take_third(3)
-    take_third(2)
+    ring_step(4)
     attend_shared(0)
 
     @pl.when(has_lane(3))
     def _():
-        @pl.when(p == 0)
-        def _():
-            hop(2, NB - 1).wait_recv()
-
+        hop(2, NB - 1).wait_recv()
         scores = lax.dot_general(qb[:BLK, :], kv[3, NB - 1, 0], NT, preferred_element_type=F32)
         half = scores * scale
         kept = half * mr[0, 3 * 6 + 2 : 3 * 6 + 3, BLK:]
@@ -370,8 +388,6 @@
         att[:BLK, :] += jnp.dot(weight, kv[3, NB - 1, 1], preferred_element_type=F32)
 
     finish(0)
-    take_third(1)
-    take_third(0)
     for r in range(1, n_up + 1):
         share_up(r, 1 - p).wait_recv()
     for r in range(1, n_down + 1):
@@ -379,23 +395,34 @@
     mix(1)
     mix(0)
 
-    for l in range(3):
-
-        @pl.when(has_lane(l) & ~is_last)
-        def _():
-            for i in range(NB):
-                if l < 2 or i == NB - 1:
-                    hop(l, i).wait_send()
-                else:
-
-                    @pl.when(p == 1)
-                    def _():
-                        hop(l, i).wait_send()
-
-        @pl.when(has_lane(l + p))
-        def _():
-            for i in range(NB):
-                push(l, i).wait_send()
+    def sent(i, carry):
+        for l in range(2):
+
+            @pl.when(has_lane(l) & ~is_last)
+            def _():
+                hop(l, i).wait_send()
+
+        @pl.when(has_lane(2) & ~is_last & (p == 1))
+        def _():
+            third(i).wait_send()
+
+        for k in range(3):
+
+            @pl.when(has_lane(k + p) & (k + p <= 2))
+            def _():
+                push(k, i).wait_send()
+
+        return carry
+
+    lax.fori_loop(0, NB, sent, 0)
+
+    @pl.when(has_lane(2) & ~is_last & (p == 0))
+    def _():
+        hop(2, NB - 1).wait_send()
+
+    @pl.when(has_lane(3) & (p == 0))
+    def _():
+        third_shared.wait_send()
 
     for r in range(1, n_up + 1):
         ring_up(r).wait_send()
@@ -425,7 +452,7 @@
             functools.partial(kernel, S, Y, NB),
             out_shape=jax.ShapeDtypeStruct((NB, Y, BLK // Y, cols), BF16),
             in_specs=[hbm, vmem, hbm, vmem, hbm, pl.BlockSpec(memory_space=pltpu.SMEM)],
-            out_specs=hbm,
+            out_specs=vmem,
             scratch_shapes=[
                 pltpu.VMEM((tok, width), BF16),
                 pltpu.VMEM((tok, width), BF16),
@@ -445,14 +472,19 @@
                 dma((3, NB)), dma((3, NB)), dma((3, NB)), dma((3, NB)),
                 dma((Y,)), dma((Y,)), dma((Y,)), dma((Y,)),
                 dma((Y,)), dma((Y,)), dma((Y,)), dma((Y,)),
-                dma((2, Y)), dma((2, Y)), dma((2, Y)), dma((2, Y)),
+                dma((2, Y)), dma((2, Y)), dma((2, Y)), dma((2, Y)), dma((1,)),
             ],
             compiler_params=pltpu.CompilerParams(
-                collective_id=0, has_side_effects=True, vmem_limit_bytes=56 * 2**20
+                collective_id=0, has_side_effects=True, vmem_limit_bytes=40 * 2**20
             ),
         )(
-            history, ln_gain, w_in, out_gain,
-            w_out.reshape(2, DH // 2, width), block_lists,
+            *(
+                pltpu.with_memory_space_constraint(x, pltpu.HBM)
+                for x in (
+                    history, ln_gain, w_in, out_gain,
+                    w_out.reshape(2, DH // 2, width), block_lists,
+                )
+            )
         ).reshape(tok, cols)
 
     placed = (

time: 54.8 us -> 54.1 us (0.987)
  the two profiles are of different devices: /device:TPU:16 before, /device:TPU:2 now
where the time goes in v3:
time: 54.1 us; the launch traced here: 53.9 us
  Pallas kernels  53.3 us (99%)
  local copies, waits for them, and re-layouts  0.68 us (1%)
    pallas_call x1, Pallas kernels, body(): pl.pallas_call(functools.partial(kernel, S, Y, NB), out_shape=jax.ShapeDt...  53.3 us

profile of v3, /device:TPU:2, one launch (start us, length us, event | category | flops | bytes accessed | tf_op | source)
XLA Modules:
  0.0 53.9 jit_solution(2577123911019615132)
XLA Ops:
  0.0 53.3 %shard_map.64 = bf16[6,8,16,128]{3,2,1,0:T(8,128)(2,1)S(1)} custom-call(bf16[768,1024]{1,0:T(8,128)(2,1)} %hist.1, bf16[1024]{0:T(1024)(128)(2,1)} %lng.1, bf16[4,1024,128]{2,1,0:T(8,128)(2,1)} %win.1, bf16[128]{0:T(256)(128)(2,1)} %og.1, bf16[2,64,1024]{2,1,0:T(8,128)(2,1)} %bitcast.3, s32[6,16]{1,0:T(8,128)} %lists.1), custom_call_target="tpu_custom_call" | custom-call | tf_op jit(solution)/shard_map/pallas_call | solution.py:451
  53.3 0.7 %copy.8 = bf16[768,128]{1,0:T(8,128)(2,1)} copy(bf16[768,128]{1,0:T(8,128)(2,1)S(1)} %bitcast.2) | data formatting | bytes 393216

commit v4 on v3

--- a/solution.py
+++ b/solution.py
@@ -25,7 +25,7 @@
     S, Y, NB,
     hist, lng, win, og, wout, lists, o_ref,
     xb, nb, wkv, wqg, wf, kv, sv, qb, gb, att, mr, gat, gall, ob,
-    in_sem, w_sem, xs, xr, ps, pr, rs, rr, ls, lr, bs, br, cs, cr, a1s, a1r, a2s, a2r, fs,
+    in_sem, w_sem, xs, xr, ps, pr, rs, rr, ls, lr, bs, br, a1s, a1r, a2s, a2r, fs,
 ):
     share = BLK // Y
     s = lax.axis_index("seq")
@@ -106,62 +106,54 @@
         device_id={"seq": sib}, device_id_type=MESH,
     )
 
-    up = lax.rem(h + 1, Y)
-    down = lax.rem(h + Y - 1, Y)
-
-    def ring_up(r):
-        at = lax.rem(h - r + 1 + Y, Y)
-        return pltpu.make_async_remote_copy(
-            src_ref=wf.at[at, p], dst_ref=wf.at[at, p],
-            send_sem=rs.at[r], recv_sem=rr.at[r],
-            device_id={"head": up}, device_id_type=MESH,
-        )
-
-    def ring_down(r):
-        at = lax.rem(h + r - 1, Y)
-        return pltpu.make_async_remote_copy(
-            src_ref=wf.at[at, p], dst_ref=wf.at[at, p],
-            send_sem=ls.at[r], recv_sem=lr.at[r],
-            device_id={"head": down}, device_id_type=MESH,
-        )
-
-    def share_up(r, half):
-        at = lax.rem(h - r + Y, Y)
-        return pltpu.make_async_remote_copy(
-            src_ref=wf.at[at, half], dst_ref=wf.at[at, half],
-            send_sem=bs.at[r], recv_sem=br.at[r],
+    def place(k):
+        return lax.rem(h + k + Y, Y)
+
+    near = (1, -1, 2, -2)
+
+    def gather_near(n):
+        return pltpu.make_async_remote_copy(
+            src_ref=wf.at[h, p], dst_ref=wf.at[h, p],
+            send_sem=rs.at[n], recv_sem=rr.at[n],
+            device_id={"head": place(near[n])}, device_id_type=MESH,
+        )
+
+    def gather_far(n):
+        sign = 1 if n % 2 == 0 else -1
+        shard = wf.at[place(-2 * sign), p]
+        if n >= 2:
+            shard = shard.at[pl.ds((n - 2) * (half_rows // 2), half_rows // 2)]
+        return pltpu.make_async_remote_copy(
+            src_ref=shard, dst_ref=shard,
+            send_sem=ls.at[n], recv_sem=lr.at[n],
+            device_id={"head": place(sign if n < 2 else 2 * sign)}, device_id_type=MESH,
+        )
+
+    def share_half(k, half):
+        shard = wf.at[place(k), half]
+        return pltpu.make_async_remote_copy(
+            src_ref=shard, dst_ref=shard,
+            send_sem=bs.at[k], recv_sem=br.at[k],
             device_id={"seq": sib}, device_id_type=MESH,
         )
 
-    def share_down(r, half):
-        at = lax.rem(h + r, Y)
-        return pltpu.make_async_remote_copy(
-            src_ref=wf.at[at, half], dst_ref=wf.at[at, half],
-            send_sem=cs.at[r], recv_sem=cr.at[r],
-            device_id={"seq": sib}, device_id_type=MESH,
-        )
-
-    n_up = Y // 2
-    n_down = Y - 1 - n_up
-
-    def ring_step(n):
-        @pl.when((n >= 1) & (n <= n_up))
-        def _():
-            ring_up(n).wait_recv()
-            share_up(n, p).start()
-
-        @pl.when((n >= 1) & (n <= n_down))
-        def _():
-            ring_down(n).wait_recv()
-            share_down(n, p).start()
-
-        @pl.when(n + 1 <= n_up)
-        def _():
-            ring_up(n + 1).start()
-
-        @pl.when(n + 1 <= n_down)
-        def _():
-            ring_down(n + 1).start()
+    def gather_start():
+        for n in range(4):
+            gather_near(n).start()
+
+    def gather_middle():
+        for n in range(4):
+            gather_near(n).wait_recv()
+        for n in range(4):
+            gather_far(n).start()
+        for k in (1, 2, Y - 1, Y - 2):
+            share_half(k, p).start()
+
+    def gather_end():
+        for n in range(4):
+            gather_far(n).wait_recv()
+        for k in (3, 4, 5):
+            share_half(k, p).start()
 
     loads[0].wait()
     loads[1].wait()
@@ -195,7 +187,7 @@
         @pl.when(n == 0)
         def _():
             load_out.wait()
-            ring_step(0)
+            gather_start()
 
         return carry
 
@@ -289,9 +281,9 @@
             keys, values = pair(sv, l - 1, t)
             attend(keys, values, 3 * (2 * l - 1) + t, 0, None)
 
-        @pl.when(lax.rem(n, 2) == 1)
-        def _():
-            ring_step((n + 1) // 2)
+        @pl.when(n == 3)
+        def _():
+            gather_middle()
 
         return carry
 
@@ -375,7 +367,7 @@
     attend_shared(2)
     attend_shared(1)
     finish(1)
-    ring_step(4)
+    gather_end()
     attend_shared(0)
 
     @pl.when(has_lane(3))
@@ -388,10 +380,8 @@
         att[:BLK, :] += jnp.dot(weight, kv[3, NB - 1, 1], preferred_element_type=F32)
 
     finish(0)
-    for r in range(1, n_up + 1):
-        share_up(r, 1 - p).wait_recv()
-    for r in range(1, n_down + 1):
-        share_down(r, 1 - p).wait_recv()
+    for k in range(1, Y):
+        share_half(k, 1 - p).wait_recv()
     mix(1)
     mix(0)
 
@@ -424,12 +414,11 @@
     def _():
         third_shared.wait_send()
 
-    for r in range(1, n_up + 1):
-        ring_up(r).wait_send()
-        share_up(r, p).wait_send()
-    for r in range(1, n_down + 1):
-        ring_down(r).wait_send()
-        share_down(r, p).wait_send()
+    for n in range(4):
+        gather_near(n).wait_send()
+        gather_far(n).wait_send()
+    for k in range(1, Y):
+        share_half(k, p).wait_send()
     for part in range(2):
         keep_columns(part).wait()
         for k in range(1, Y):
@@ -470,8 +459,7 @@
                 pltpu.VMEM((Y, NB, BLK // Y, cols), BF16),
                 dma((NB,)), dma((5,)),
                 dma((3, NB)), dma((3, NB)), dma((3, NB)), dma((3, NB)),
-                dma((Y,)), dma((Y,)), dma((Y,)), dma((Y,)),
-                dma((Y,)), dma((Y,)), dma((Y,)), dma((Y,)),
+                dma((4,)), dma((4,)), dma((4,)), dma((4,)), dma((Y,)), dma((Y,)),
                 dma((2, Y)), dma((2, Y)), dma((2, Y)), dma((2, Y)), dma((1,)),
             ],
             compiler_params=pltpu.CompilerParams(

time: 54.1 us -> 46.8 us (0.87)
  Pallas kernels: 53.3 us -> 45.9 us
    pallas_call x1, Pallas kernels: 53.3 us -> 45.9 us  [body(): pl.pallas_call(functools.partial(kernel, S, Y, NB), out_shape=jax.ShapeDt...]
where the time goes in v4:
time: 46.8 us; the launch traced here: 46.6 us
  Pallas kernels  45.9 us (98%)
  local copies, waits for them, and re-layouts  0.68 us (1%)
    pallas_call x1, Pallas kernels, body(): pl.pallas_call(functools.partial(kernel, S, Y, NB), out_shape=jax.ShapeDt...  45.9 us

profile of v4, /device:TPU:2, one launch (start us, length us, event | category | flops | bytes accessed | tf_op | source)
XLA Modules:
  0.0 46.6 jit_solution(919647913002276952)
XLA Ops:
  0.0 45.9 %shard_map.64 = bf16[6,8,16,128]{3,2,1,0:T(8,128)(2,1)S(1)} custom-call(bf16[768,1024]{1,0:T(8,128)(2,1)} %hist.1, bf16[1024]{0:T(1024)(128)(2,1)} %lng.1, bf16[4,1024,128]{2,1,0:T(8,128)(2,1)} %win.1, bf16[128]{0:T(256)(128)(2,1)} %og.1, bf16[2,64,1024]{2,1,0:T(8,128)(2,1)} %bitcast.3, s32[6,16]{1,0:T(8,128)} %lists.1), custom_call_target="tpu_custom_call" | custom-call | tf_op jit(solution)/shard_map/pallas_call | solution.py:440
  45.9 0.7 %copy.8 = bf16[768,128]{1,0:T(8,128)(2,1)} copy(bf16[768,128]{1,0:T(8,128)(2,1)S(1)} %bitcast.2) | data formatting | bytes 393216
